TPU v7x, 256 devices: a whole 4x4x8 slice. The times are simulated.
256 devices in a mesh: lon: 32 (over y_lo, z, core), lat: 8 (over x, y_hi).
Axes of the slice: x: 4, y: 4 (y_hi: 2, y_lo: 2; y = y_hi * 2 + y_lo), z: 8, core: 2. Of those that a mesh axis runs over, the one named last changes fastest.
Arguments:
- perturbations: float32 [2, 16, 1024, 4096], P(None, None, 'lat', 'lon'), may hold values from -6 to 6
- zonal_rate: float32 [2, 2, 4096], P(None, None, 'lon'), may hold values from 0.5 to 1, as said below
- meridional_rate: float32 [2, 2, 1024], replicated, may hold values from 0.5 to 1, as said below
- amplitude: float32 [2, 2, 1024, 4096], P(None, None, 'lat', 'lon'), may hold values from 1 to 10
Outputs:
- localized: float32 [2, 16, 1024, 4096], P(None, None, 'lat', 'lon')
Inputs may be any that keep to these rules, and one draw needn't show every extreme that they name: `zonal_rate`: every entry is greater than 0.5 and at most 1 - 0.15 / 4096. `meridional_rate`: every entry is greater than 0.5 and at most 1 - 0.15 / 1024.
All inputs are finite; a program needn't handle non-finite values.
Results may differ from a plain program's by a relative error of at most 0.0003.
Values sent between devices are 32-bit elements; how exact they have to be, the bound alone decides.
A program may use at most 64 MiB of HBM per device.

v0:
```python
import functools

import jax
import jax.numpy as jnp
from jax import lax
from jax.experimental import pallas as pl
from jax.experimental.pallas import tpu as pltpu
from jax.sharding import PartitionSpec as P

MESH = pl.DeviceIdType.MESH
F32, BF16 = jnp.float32, jnp.bfloat16
HIGHEST = lax.Precision.HIGHEST

NN = (((1,), (0,)), ((), ()))
NT = (((1,), (1,)), ((), ()))
TN = (((0,), (0,)), ((), ()))


def halves(x):
    high = x.astype(BF16)
    return high, (x - high.astype(F32)).astype(BF16)


def mul(a, b, dims):
    return lax.dot_general(a, b, dims, preferred_element_type=F32)


def dot3(a, b, dims):
    ah, al = halves(a)
    bh, bl = halves(b)
    ka, kb = dims[0][0][0], dims[0][1][0]
    return mul(jnp.concatenate([ah, al], ka), jnp.concatenate([bh, bh], kb), dims) + mul(
        ah, bl, dims
    )


def lane(shape):
    return lax.broadcasted_iota(jnp.int32, shape, 1)


def row(shape):
    return lax.broadcasted_iota(jnp.int32, shape, 0)


def scan_lanes(v, steps, sign):
    width = v.shape[1]
    for k, factor in steps:
        v = v + factor * pltpu.roll(v, k if sign > 0 else width - k, 1)
    return v


def solve(states, coupling, blocks, cyclic):
    g, r, e1e2, w1e2, e1w2, w1w2 = coupling
    shape = (blocks, 128)
    at = row(shape)
    levels = blocks.bit_length() - 1

    def shifted(x, k):
        moved = pltpu.roll(x, k % blocks, 0)
        if cyclic:
            return moved
        return jnp.where((at >= k) if k > 0 else (at < blocks + k), moved, 0.0)

    factors = {}
    for sign in (1, -1):
        a = pltpu.roll(g, sign % blocks, 0)
        factors[sign] = []
        for level in range(levels):
            factors[sign].append(a)
            a = a * pltpu.roll(a, (sign * 2**level) % blocks, 0)
        factors[sign].append(1.0 / (1.0 - a) if cyclic else None)

    def carry(parts, sign):
        out = []
        for v in parts:
            v = shifted(v, sign)
            for level in range(levels):
                v = v + factors[sign][level] * shifted(v, sign * 2**level)
            out.append(v * factors[sign][levels] if cyclic else v)
        return out

    n = len(states[0])
    e1 = carry(states[0], 1)
    w1 = carry([states[1][i] + r * e1[i] for i in range(n)], -1)
    e2 = carry([states[2][i] + e1e2 * e1[i] + w1e2 * w1[i] for i in range(n)], 1)
    w2 = carry(
        [states[3][i] + e1w2 * e1[i] + w1w2 * w1[i] + r * e2[i] for i in range(n)], -1
    )
    return e1, w1, e2, w2


def kernel(
    nz, nm, mem, split1, split2,
    x_hbm, zr_ref, mr_ref, amp_hbm, out_ref,
    x_ref, amp_ref, field,
    vz_ref, vm_ref, uz_ref, um_ref,
    az_wide, az_low, am_wide, am_low,
    qs, qr, rs, rin, ps, pr, prs, pin,
    kz_own, kz_all, km_own, km_all, crs, crr, centre,
    lq_ref, d_ref, cr_tile,
    load_sem, send_sem, recv_sem,
):
    zi, mi = lax.axis_index("lon"), lax.axis_index("lat")
    rows = 16 * mem
    zrows, mrows = rows // nz, rows // nm
    per_pair = 4 * mem

    barrier = pltpu.get_barrier_semaphore()

    def greet_lon(k, _):
        pl.semaphore_signal(
            barrier, inc=1, device_id={"lon": lax.rem(zi + k, nz)}, device_id_type=MESH
        )
        return 0

    def greet_lat(k, _):
        pl.semaphore_signal(
            barrier, inc=1, device_id={"lat": lax.rem(mi + k, nm)}, device_id_type=MESH
        )
        return 0

    lax.fori_loop(1, nz, greet_lon, 0)
    lax.fori_loop(1, nm, greet_lat, 0)
    x_copy = pltpu.make_async_copy(x_hbm, x_ref, load_sem.at[0])
    amp_copy = pltpu.make_async_copy(amp_hbm, amp_ref, load_sem.at[1])
    x_copy.start()
    amp_copy.start()

    own = pl.ds(pl.multiple_of(mi * 128, 128), 128)
    a = jnp.concatenate(
        [zr_ref[0], zr_ref[1], mr_ref[0, :, own], mr_ref[1, :, own]], axis=0
    )
    loss = 1.0 - a
    la = jnp.log(a)
    square = (128, 128)
    upto = jnp.where(row(square) <= lane(square), 1.0, 0.0)
    li = lax.dot_general(la, upto, NN, precision=HIGHEST, preferred_element_type=F32)
    lx = li - la
    total = li[:, 127:128]
    at = lane((8, 128))
    east_cols, west_cols, east_rows, west_rows = [], [], [], []
    for p in range(7):
        k = 2**p
        back = pltpu.roll(li, k, 1)
        ahead = pltpu.roll(li, 128 - k, 1)
        xback = pltpu.roll(lx, k, 1)
        xahead = pltpu.roll(lx, 128 - k, 1)
        first, last = at >= k, at < 128 - k
        east_cols.append((k, jnp.where(first, jnp.exp(jnp.where(first, li - back, 0.0)), 0.0)))
        east_rows.append((k, jnp.where(last, jnp.exp(jnp.where(last, ahead - li, 0.0)), 0.0)))
        west_cols.append((k, jnp.where(last, jnp.exp(jnp.where(last, xahead - lx, 0.0)), 0.0)))
        west_rows.append((k, jnp.where(first, jnp.exp(jnp.where(first, lx - xback, 0.0)), 0.0)))

    def rows_east(v):
        return loss * scan_lanes(v, east_rows, -1)

    def rows_west(v):
        return loss * scan_lanes(v, west_rows, 1)

    def cols_east(x):
        return scan_lanes(loss * x, east_cols, 1)

    def cols_west(x):
        return scan_lanes(loss * x, west_cols, -1)

    ge = jnp.exp(li)
    gw = jnp.exp(total - lx)
    v1 = jnp.exp(total - li) * loss
    w0 = jnp.exp(lx) * loss
    v2 = rows_east(w0)
    x1 = rows_west(v1)
    v3 = rows_east(x1)
    x2 = rows_west(v2)
    v4 = rows_east(x2)

    def along(v):
        return jnp.sum(v, axis=1, keepdims=True)

    kinds = (
        jnp.exp(total), along(w0 * ge), along(x1 * ge),
        along(v1 * gw), along(x2 * ge), along(v2 * gw),
    )
    packed = jnp.zeros((8, 128), F32)
    for k, value in enumerate(kinds):
        packed = jnp.where(at == k, value, packed)
    for n in range(4):
        kz_own[n] = packed[n : n + 1]
    km_own[0:4] = packed[4:8]
    km_own[4:8] = packed[4:8]
    for f, v in enumerate((v1, v2, v3, v4)):
        for n in range(4):
            vz_ref[n * 4 + f : n * 4 + f + 1, :] = v[n : n + 1]
            vm_ref[n * 4 + f : n * 4 + f + 1, :] = v[4 + n : 5 + n]

    x_copy.wait()
    for l in range(2):
        both = [
            jnp.concatenate([ref[l * 4 : l * 4 + 4], ref[8 + l * 4 : 12 + l * 4]], axis=0)
            for ref in (vz_ref, vm_ref)
        ]
        zh, zl = halves(both[0])
        mh, ml = halves(both[1])
        z_wide = jnp.concatenate([zh, zl], axis=1)
        m_wide = jnp.concatenate([mh, ml], axis=1)

        def states(m, _):
            xh, xl = halves(x_ref[l, m])
            q = mul(z_wide, jnp.concatenate([xh, xh], axis=1), NT) + mul(zh, xl, NT)
            p = mul(m_wide, jnp.concatenate([xh, xh], axis=0), NN) + mul(mh, xl, NN)
            for s in range(2):
                base = (s * 2 + l) * per_pair
                qs[pl.ds(base + m * 4, 4), :] = q[s * 4 : s * 4 + 4]
                ps[pl.ds(base + m * 4, 4), :] = p[s * 4 : s * 4 + 4]
            return 0

        lax.fori_loop(0, mem, states, 0, unroll=4)

    pl.semaphore_wait(barrier, nz + nm - 2)

    def chunk(ref, index, size):
        return ref.at[pl.ds(pl.multiple_of(index * size, size), size), :]

    def remote(src, dst, which, **device):
        return pltpu.make_async_remote_copy(
            src_ref=src, dst_ref=dst,
            send_sem=send_sem.at[which], recv_sem=recv_sem.at[which],
            device_id=device, device_id_type=MESH,
        )

    other_z, other_m = lax.rem(zi + 1, nz), lax.rem(mi + 1, nm)

    def send_lon(k, _):
        d = lax.rem(zi + k, nz)
        remote(kz_own.at[d * zrows // per_pair], kz_all.at[zi], 1, lon=d).start()
        remote(chunk(qs, d, zrows), chunk(qr, zi, zrows), 0, lon=d).start()
        return 0

    def send_lat(k, _):
        d = lax.rem(mi + k, nm)
        remote(chunk(ps, d, mrows), chunk(pr, mi, mrows), 2, lat=d).start()
        remote(km_own, chunk(km_all, mi, 8), 3, lat=d).start()
        return 0

    lax.fori_loop(1, nz, send_lon, 0)
    lax.fori_loop(1, nm, send_lat, 0)
    kz_all[zi] = kz_own[zi * zrows // per_pair]
    chunk(qr, zi, zrows)[...] = chunk(qs, zi, zrows)[...]
    chunk(pr, mi, mrows)[...] = chunk(ps, mi, mrows)[...]
    chunk(km_all, mi, 8)[...] = km_own[...]

    u3 = cols_west(ge)
    u2 = cols_west(cols_east(gw))
    u1 = cols_west(cols_east(u3))
    for f, u in enumerate((u1, u2, u3, gw)):
        for n in range(4):
            uz_ref[n * 4 + f : n * 4 + f + 1, :] = u[n : n + 1]
            um_ref[n * 4 + f : n * 4 + f + 1, :] = u[4 + n : 5 + n]

    lit, lxt = jnp.transpose(li), jnp.transpose(lx)
    below = row(square) >= lane(square)
    above = row(square) <= lane(square)
    for n in range(8):
        down = jnp.where(below, lit[:, n : n + 1] - li[n : n + 1], 0.0)
        up = jnp.where(above, lx[n : n + 1] - lxt[:, n : n + 1], 0.0)
        east = jnp.where(below, jnp.exp(down), 0.0) * loss[n : n + 1]
        west = jnp.where(above, jnp.exp(up), 0.0) * loss[n : n + 1]
        once = dot3(west, east, NN)
        high, low = halves(dot3(once, once, NN))
        if n < 4:
            s, l = n // 2, n % 2
            az_wide[l, s * 128 : s * 128 + 128, 0:128] = high
            az_wide[l, s * 128 : s * 128 + 128, 128:256] = high
            az_low[l, s * 128 : s * 128 + 128, :] = low
        else:
            am_wide[n - 4, :, 0:128] = high
            am_wide[n - 4, :, 128:256] = high
            am_low[n - 4] = low

    def local_pass(i, _):
        l, m = i // mem, lax.rem(i, mem)
        xh, xl = halves(x_ref[l, m])
        f = mul(jnp.concatenate([xh, xl], axis=1), az_wide[l], NT) + mul(xh, az_low[l], NT)
        for s in range(2):
            n = s * 2 + l
            fh, fl = halves(f[:, s * 128 : s * 128 + 128])
            field[n, m] = mul(am_wide[n], jnp.concatenate([fh, fl], axis=0), NN) + mul(
                am_low[n], fh, NN
            )
        return 0

    lax.fori_loop(0, split1, local_pass, 0, unroll=2)

    zshape, mshape = (nz, 128), (nm, 128)
    remote(qs.at[pl.ds(0, (nz - 1) * zrows)], qr.at[pl.ds(0, (nz - 1) * zrows)], 0, lon=other_z).wait()
    remote(kz_all.at[pl.ds(0, nz - 1)], kz_all.at[pl.ds(0, nz - 1)], 1, lon=other_z).wait()
    kz = kz_all[...].reshape(nz, 128)
    coupling = [jnp.broadcast_to(kz[:, k : k + 1], zshape) for k in range(6)]
    groups = zrows // 4
    got = [
        [qr[pl.ds(g * 4 + f, nz, stride=zrows), :] for g in range(groups)] for f in range(4)
    ]
    for f, parts in enumerate(solve(got, coupling, nz, True)):
        for g in range(groups):
            rs[pl.ds(g * 4 + f, nz, stride=zrows), :] = parts[g]

    def back_lon(k, _):
        d = lax.rem(zi + k, nz)
        remote(chunk(rs, d, zrows), chunk(rin, zi, zrows), 4, lon=d).start()
        return 0

    lax.fori_loop(1, nz, back_lon, 0)
    chunk(rin, zi, zrows)[...] = chunk(rs, zi, zrows)[...]

    remote(ps.at[pl.ds(0, (nm - 1) * mrows)], pr.at[pl.ds(0, (nm - 1) * mrows)], 2, lat=other_m).wait()
    remote(km_all.at[pl.ds(0, (nm - 1) * 8)], km_all.at[pl.ds(0, (nm - 1) * 8)], 3, lat=other_m).wait()
    pair = mi * mrows // per_pair
    km = [km_all[pl.ds(n, nm, stride=8), :] for n in range(4)]
    mine = km[0]
    for n in range(1, 4):
        mine = jnp.where(pair == n, km[n], mine)
    coupling = [jnp.broadcast_to(mine[:, k : k + 1], mshape) for k in range(6)]
    groups = mrows // 4
    got = [
        [pr[pl.ds(g * 4 + f, nm, stride=mrows), :] for g in range(groups)] for f in range(4)
    ]
    for f, parts in enumerate(solve(got, coupling, nm, False)):
        for g in range(groups):
            prs[pl.ds(g * 4 + f, nm, stride=mrows), :] = parts[g]

    def back_lat(k, _):
        d = lax.rem(mi + k, nm)
        remote(chunk(prs, d, mrows), chunk(pin, mi, mrows), 5, lat=d).start()
        return 0

    lax.fori_loop(1, nm, back_lat, 0)
    chunk(pin, mi, mrows)[...] = chunk(prs, mi, mrows)[...]

    lax.fori_loop(split1, split2, local_pass, 0, unroll=2)

    remote(rs.at[pl.ds(0, (nz - 1) * zrows)], rin.at[pl.ds(0, (nz - 1) * zrows)], 4, lon=other_z).wait()
    cross = dot3(vm_ref[...], rin[...], NT)
    wide = (16, rows)
    cross = jnp.where(row(wide) // 4 == lane(wide) // per_pair, cross, 0.0)
    cross = cross[0:4] + cross[4:8] + cross[8:12] + cross[12:16]
    crs[0:4] = cross[:, 0:128]
    crs[4:8] = cross[:, 128:256]

    def send_cross(k, _):
        d = lax.rem(mi + k, nm)
        remote(crs, chunk(crr, mi, 8), 6, lat=d).start()
        return 0

    lax.fori_loop(1, nm, send_cross, 0)
    chunk(crr, mi, 8)[...] = crs[...]

    lax.fori_loop(split2, 2 * mem, local_pass, 0, unroll=2)

    remote(prs.at[pl.ds(0, (nm - 1) * mrows)], pin.at[pl.ds(0, (nm - 1) * mrows)], 5, lat=other_m).wait()
    for n in range(4):
        s, l = n // 2, n % 2
        part = slice(n * per_pair, (n + 1) * per_pair)
        ph, plow = halves(pin[part])
        d_ref[part] = mul(
            jnp.concatenate([ph, plow], axis=1), az_wide[l, s * 128 : s * 128 + 128, :], NT
        ) + mul(ph, az_low[l, s * 128 : s * 128 + 128, :], NT)
        qh, ql = halves(rin[part])
        lq_ref[part] = mul(jnp.concatenate([qh, ql], axis=1), am_wide[n], NT) + mul(
            qh, am_low[n], NT
        )
    amp_copy.wait()

    remote(crr.at[pl.ds(0, (nm - 1) * 8)], crr.at[pl.ds(0, (nm - 1) * 8)], 6, lat=other_m).wait()
    for h in range(2):
        left = lane(mshape) < per_pair
        coupling = [
            jnp.where(left, km[2 * h][:, k : k + 1], km[2 * h + 1][:, k : k + 1])
            for k in range(6)
        ]
        got = [[crr[pl.ds(h * 4 + f, nm, stride=8), :]] for f in range(4)]
        for f, parts in enumerate(solve(got, coupling, nm, False)):
            centre[h * 4 + f] = parts[0]
    for n in range(4):
        h = n // 2
        for f in range(4):
            line = centre[h * 4 + f, pl.ds(mi, 1), :]
            line = jnp.where(lane((1, 128)) // per_pair == n % 2, line, 0.0)
            r = n * 4 + f
            cr_tile[r : r + 1, h * 128 : h * 128 + 128] = line
            cr_tile[r : r + 1, (1 - h) * 128 : (1 - h) * 128 + 128] = jnp.zeros((1, 128), F32)
    lq_ref[...] += dot3(cr_tile[...], um_ref[...], TN)

    def finish(i, _):
        l, m = i // mem, lax.rem(i, mem)
        result = None
        for s in range(2):
            n = s * 2 + l
            part = pl.ds(n * per_pair + m * 4, 4)
            resp = pl.ds(n * 4, 4)
            left = jnp.concatenate([lq_ref[part, :], um_ref[resp, :]], axis=0)
            right = jnp.concatenate([uz_ref[resp, :], d_ref[part, :]], axis=0)
            lh = left.astype(BF16).astype(F32)
            rh = right.astype(BF16).astype(F32)
            stacked_left = jnp.concatenate([lh, left - lh, lh], axis=0).astype(BF16)
            stacked_right = jnp.concatenate([rh, rh, right - rh], axis=0).astype(BF16)
            y = field[n, m] + mul(stacked_left, stacked_right, TN)
            y = y * amp_ref[s, l]
            result = y if result is None else result + y
        out_ref[l, m] = result
        return 0

    lax.fori_loop(0, 2 * mem, finish, 0, unroll=4)


def body(nz, nm, perturbations, zonal_rate, meridional_rate, amplitude):
    mem = perturbations.shape[1]
    rows = 16 * mem
    vmem = pltpu.VMEM
    split1, split2 = 12, 24
    return pl.pallas_call(
        functools.partial(kernel, nz, nm, mem, split1, split2),
        out_shape=jax.ShapeDtypeStruct(perturbations.shape, F32),
        in_specs=[
            pl.BlockSpec(memory_space=pl.ANY),
            pl.BlockSpec(memory_space=pltpu.VMEM),
            pl.BlockSpec(memory_space=pltpu.VMEM),
            pl.BlockSpec(memory_space=pl.ANY),
        ],
        out_specs=pl.BlockSpec(memory_space=pltpu.VMEM),
        scratch_shapes=[
            vmem((2, mem, 128, 128), F32),
            vmem((2, 2, 128, 128), F32),
            vmem((4, mem, 128, 128), F32),
            vmem((16, 128), F32), vmem((16, 128), F32),
            vmem((16, 128), F32), vmem((16, 128), F32),
            vmem((2, 256, 256), BF16), vmem((2, 256, 128), BF16),
            vmem((4, 128, 256), BF16), vmem((4, 128, 128), BF16),
            *[vmem((rows, 128), F32) for _ in range(8)],
            vmem((4, 1, 128), F32), vmem((nz, 1, 128), F32),
            vmem((8, 128), F32), vmem((8 * nm, 128), F32),
            vmem((8, 128), F32), vmem((8 * nm, 128), F32),
            vmem((8, nm, 128), F32),
            vmem((rows, 128), F32), vmem((rows, 128), F32), vmem((16, 256), F32),
            pltpu.SemaphoreType.DMA((2,)),
            pltpu.SemaphoreType.DMA((7,)),
            pltpu.SemaphoreType.DMA((7,)),
        ],
        compiler_params=pltpu.CompilerParams(
            collective_id=0, has_side_effects=True, vmem_limit_bytes=48 * 1024 * 1024
        ),
    )(perturbations, zonal_rate, meridional_rate, amplitude)


def solution(mesh):
    spec = P(None, None, "lat", "lon")
    return jax.shard_map(
        functools.partial(body, mesh.shape["lon"], mesh.shape["lat"]),
        mesh=mesh,
        in_specs=(spec, P(None, None, "lon"), P(), spec),
        out_specs=spec,
        check_vma=False,
    )
```

profile of v0, /device:TPU:1, one launch (start us, length us, event | category | flops | bytes accessed | tf_op | source)
XLA Modules:
  0.0 38.5 jit_solution(5981753422071775036)
XLA Ops:
  0.0 0.0 copy-start
  0.0 1.6 %copy-done = f32[2,16,128,128]{3,2,1,0:T(8,128)S(1)} copy-done((f32[2,16,128,128]{3,2,1,0:T(8,128)S(1)}, f32[2,16,128,128]{3,2,1,0:T(8,128)}, u32[]{:S(2)}) %copy-start) | copy-done | bytes 2097176
  1.6 0.0 copy-start.1
  1.6 0.9 %copy-done.1 = f32[2,2,128,128]{3,2,1,0:T(8,128)S(1)} copy-done((f32[2,2,128,128]{3,2,1,0:T(8,128)S(1)}, f32[2,2,128,128]{3,2,1,0:T(8,128)}, u32[]{:S(2)}) %copy-start.1) | copy-done | bytes 262168
  2.5 0.0 copy-start.2
  2.5 0.7 %copy-done.2 = f32[2,2,1024]{2,1,0:T(2,128)S(1)} copy-done((f32[2,2,1024]{2,1,0:T(2,128)S(1)}, f32[2,2,1024]{2,1,0:T(2,128)}, u32[]{:S(2)}) %copy-start.2) | copy-done | bytes 16408
  3.3 0.0 copy-start.3
  3.3 0.7 %copy-done.3 = f32[2,2,128]{2,1,0:T(2,128)S(1)} copy-done((f32[2,2,128]{2,1,0:T(2,128)S(1)}, f32[2,2,128]{2,1,0:T(2,128)}, u32[]{:S(2)}) %copy-start.3) | copy-done | bytes 2072
  3.9 33.2 %shard_map.46 = f32[2,16,128,128]{3,2,1,0:T(8,128)S(1)} custom-call(f32[2,16,128,128]{3,2,1,0:T(8,128)S(1)} %copy-done, f32[2,2,128]{2,1,0:T(2,128)S(1)} %copy-done.3, f32[2,2,1024]{2,1,0:T(2,128)S(1)} %copy-done.2, f32[2,2,128,128]{3,2,1,0:T(8,128)S(1)} %copy-done.1), custom_call_target="tpu_custom_call" | custom-call | tf_op jit(solution)/shard_map/pallas_call | solution.py:419
  37.2 1.3 %copy.6 = f32[2,16,128,128]{3,2,1,0:T(8,128)} copy(f32[2,16,128,128]{3,2,1,0:T(8,128)S(1)} %shard_map.46) | data formatting | bytes 4194304
Async XLA Ops:
  0.0 1.6 %copy-start = (f32[2,16,128,128]{3,2,1,0:T(8,128)S(1)}, f32[2,16,128,128]{3,2,1,0:T(8,128)}, u32[]{:S(2)}) copy-start(f32[2,16,128,128]{3,2,1,0:T(8,128)} %x_hbm.1) | copy-start | bytes 6291460
  1.6 0.9 %copy-start.1 = (f32[2,2,128,128]{3,2,1,0:T(8,128)S(1)}, f32[2,2,128,128]{3,2,1,0:T(8,128)}, u32[]{:S(2)}) copy-start(f32[2,2,128,128]{3,2,1,0:T(8,128)} %amp_hbm.1) | copy-start | bytes 786436
  2.5 0.7 %copy-start.2 = (f32[2,2,1024]{2,1,0:T(2,128)S(1)}, f32[2,2,1024]{2,1,0:T(2,128)}, u32[]{:S(2)}) copy-start(f32[2,2,1024]{2,1,0:T(2,128)} %mr_ref.1) | copy-start | bytes 49156
  3.3 0.7 %copy-start.3 = (f32[2,2,128]{2,1,0:T(2,128)S(1)}, f32[2,2,128]{2,1,0:T(2,128)}, u32[]{:S(2)}) copy-start(f32[2,2,128]{2,1,0:T(2,128)} %zr_ref.1) | copy-start | bytes 6148
where the time goes:
time: 38.7 us; the launch traced here: 38.5 us
  Pallas kernels  33.2 us (86%)
  local copies, waits for them, and re-layouts  5.26 us (14%)
    pallas_call x1, Pallas kernels, body(): pl.pallas_call(functools.partial(kernel, nz, nm, mem, split1, split2), ou...  33.2 us
    unnamed x9, local copies, waits for them, and re-layouts  5.26 us

commit v1 on v0

--- a/solution.py
+++ b/solution.py
@@ -91,8 +91,8 @@
 
 def kernel(
     nz, nm, mem, split1, split2,
-    x_hbm, zr_ref, mr_ref, amp_hbm, out_ref,
-    x_ref, amp_ref, field,
+    x_hbm, zr_hbm, mr_hbm, amp_hbm, out_ref,
+    x_ref, zr_ref, mr_ref, amp_ref, field,
     vz_ref, vm_ref, uz_ref, um_ref,
     az_wide, az_low, am_wide, am_low,
     qs, qr, rs, rin, ps, pr, prs, pin,
@@ -119,17 +119,21 @@
         )
         return 0
 
+    own = pl.ds(pl.multiple_of(mi * 128, 128), 128)
+    zr_copy = pltpu.make_async_copy(zr_hbm, zr_ref, load_sem.at[2])
+    mr_copy = pltpu.make_async_copy(mr_hbm.at[:, :, own], mr_ref, load_sem.at[3])
+    x_copy = pltpu.make_async_copy(x_hbm, x_ref, load_sem.at[0])
+    amp_copy = pltpu.make_async_copy(amp_hbm, amp_ref, load_sem.at[1])
+    zr_copy.start()
+    mr_copy.start()
+    x_copy.start()
+    amp_copy.start()
     lax.fori_loop(1, nz, greet_lon, 0)
     lax.fori_loop(1, nm, greet_lat, 0)
-    x_copy = pltpu.make_async_copy(x_hbm, x_ref, load_sem.at[0])
-    amp_copy = pltpu.make_async_copy(amp_hbm, amp_ref, load_sem.at[1])
-    x_copy.start()
-    amp_copy.start()
-
-    own = pl.ds(pl.multiple_of(mi * 128, 128), 128)
-    a = jnp.concatenate(
-        [zr_ref[0], zr_ref[1], mr_ref[0, :, own], mr_ref[1, :, own]], axis=0
-    )
+
+    zr_copy.wait()
+    mr_copy.wait()
+    a = jnp.concatenate([zr_ref[0], zr_ref[1], mr_ref[0], mr_ref[1]], axis=0)
     loss = 1.0 - a
     la = jnp.log(a)
     square = (128, 128)
@@ -420,14 +424,12 @@
         functools.partial(kernel, nz, nm, mem, split1, split2),
         out_shape=jax.ShapeDtypeStruct(perturbations.shape, F32),
         in_specs=[
-            pl.BlockSpec(memory_space=pl.ANY),
-            pl.BlockSpec(memory_space=pltpu.VMEM),
-            pl.BlockSpec(memory_space=pltpu.VMEM),
-            pl.BlockSpec(memory_space=pl.ANY),
+            pl.BlockSpec(memory_space=pltpu.HBM) for _ in range(4)
         ],
         out_specs=pl.BlockSpec(memory_space=pltpu.VMEM),
         scratch_shapes=[
             vmem((2, mem, 128, 128), F32),
+            vmem((2, 2, 128), F32), vmem((2, 2, 128), F32),
             vmem((2, 2, 128, 128), F32),
             vmem((4, mem, 128, 128), F32),
             vmem((16, 128), F32), vmem((16, 128), F32),
@@ -440,14 +442,14 @@
             vmem((8, 128), F32), vmem((8 * nm, 128), F32),
             vmem((8, nm, 128), F32),
             vmem((rows, 128), F32), vmem((rows, 128), F32), vmem((16, 256), F32),
-            pltpu.SemaphoreType.DMA((2,)),
+            pltpu.SemaphoreType.DMA((4,)),
             pltpu.SemaphoreType.DMA((7,)),
             pltpu.SemaphoreType.DMA((7,)),
         ],
         compiler_params=pltpu.CompilerParams(
             collective_id=0, has_side_effects=True, vmem_limit_bytes=48 * 1024 * 1024
         ),
-    )(perturbations, zonal_rate, meridional_rate, amplitude)
+    )(*(pltpu.with_memory_space_constraint(v, pltpu.HBM) for v in (perturbations, zonal_rate, meridional_rate, amplitude)))
 
 
 def solution(mesh):

time: 38.7 us -> 34.9 us (0.902)
  local copies, waits for them, and re-layouts: 5.26 us -> 1.32 us
    unnamed x9 -> x1, local copies, waits for them, and re-layouts: 5.26 us -> 1.32 us
where the time goes in v1:
time: 34.9 us; the launch traced here: 34.8 us
  Pallas kernels  33.5 us (96%)
  local copies, waits for them, and re-layouts  1.32 us (4%)
    pallas_call x1, Pallas kernels, body(): pl.pallas_call(functools.partial(kernel, nz, nm, mem, split1, split2), ou...  33.5 us
    unnamed x1, local copies, waits for them, and re-layouts  1.32 us

profile of v1, /device:TPU:1, one launch (start us, length us, event | category | flops | bytes accessed | tf_op | source)
XLA Modules:
  0.0 34.8 jit_solution(5266942182689062771)
XLA Ops:
  0.0 33.5 %shard_map.46 = f32[2,16,128,128]{3,2,1,0:T(8,128)S(1)} custom-call(f32[2,16,128,128]{3,2,1,0:T(8,128)} %x_hbm.1, f32[2,2,128]{2,1,0:T(2,128)} %zr_hbm.1, f32[2,2,1024]{2,1,0:T(2,128)} %mr_hbm.1, f32[2,2,128,128]{3,2,1,0:T(8,128)} %amp_hbm.1), custom_call_target="tpu_custom_call" | custom-call | tf_op jit(solution)/shard_map/pallas_call | solution.py:423
  33.5 1.3 %copy.6 = f32[2,16,128,128]{3,2,1,0:T(8,128)} copy(f32[2,16,128,128]{3,2,1,0:T(8,128)S(1)} %shard_map.46) | data formatting | bytes 4194304

commit v2 on v1

--- a/solution.py
+++ b/solution.py
@@ -217,7 +217,7 @@
                 ps[pl.ds(base + m * 4, 4), :] = p[s * 4 : s * 4 + 4]
             return 0
 
-        lax.fori_loop(0, mem, states, 0, unroll=4)
+        lax.fori_loop(0, mem, states, 0, unroll=16)
 
     pl.semaphore_wait(barrier, nz + nm - 2)
 
@@ -292,7 +292,7 @@
             )
         return 0
 
-    lax.fori_loop(0, split1, local_pass, 0, unroll=2)
+    lax.fori_loop(0, split1, local_pass, 0, unroll=8)
 
     zshape, mshape = (nz, 128), (nm, 128)
     remote(qs.at[pl.ds(0, (nz - 1) * zrows)], qr.at[pl.ds(0, (nz - 1) * zrows)], 0, lon=other_z).wait()
@@ -339,7 +339,7 @@
     lax.fori_loop(1, nm, back_lat, 0)
     chunk(pin, mi, mrows)[...] = chunk(prs, mi, mrows)[...]
 
-    lax.fori_loop(split1, split2, local_pass, 0, unroll=2)
+    lax.fori_loop(split1, split2, local_pass, 0, unroll=8)
 
     remote(rs.at[pl.ds(0, (nz - 1) * zrows)], rin.at[pl.ds(0, (nz - 1) * zrows)], 4, lon=other_z).wait()
     cross = dot3(vm_ref[...], rin[...], NT)
@@ -357,7 +357,7 @@
     lax.fori_loop(1, nm, send_cross, 0)
     chunk(crr, mi, 8)[...] = crs[...]
 
-    lax.fori_loop(split2, 2 * mem, local_pass, 0, unroll=2)
+    lax.fori_loop(split2, 2 * mem, local_pass, 0, unroll=8)
 
     remote(prs.at[pl.ds(0, (nm - 1) * mrows)], pin.at[pl.ds(0, (nm - 1) * mrows)], 5, lat=other_m).wait()
     for n in range(4):
@@ -412,14 +412,14 @@
         out_ref[l, m] = result
         return 0
 
-    lax.fori_loop(0, 2 * mem, finish, 0, unroll=4)
+    lax.fori_loop(0, 2 * mem, finish, 0, unroll=8)
 
 
 def body(nz, nm, perturbations, zonal_rate, meridional_rate, amplitude):
     mem = perturbations.shape[1]
     rows = 16 * mem
     vmem = pltpu.VMEM
-    split1, split2 = 12, 24
+    split1, split2 = 16, 24
     return pl.pallas_call(
         functools.partial(kernel, nz, nm, mem, split1, split2),
         out_shape=jax.ShapeDtypeStruct(perturbations.shape, F32),

time: 34.9 us -> 32.5 us (0.931)
  Pallas kernels: 33.5 us -> 31.1 us
    pallas_call x1, Pallas kernels: 33.5 us -> 31.1 us  [body(): pl.pallas_call(functools.partial(kernel, nz, nm, mem, split1, split2), ou...]
where the time goes in v2:
time: 32.5 us; the launch traced here: 32.4 us
  Pallas kernels  31.1 us (96%)
  local copies, waits for them, and re-layouts  1.32 us (4%)
    pallas_call x1, Pallas kernels, body(): pl.pallas_call(functools.partial(kernel, nz, nm, mem, split1, split2), ou...  31.1 us
    unnamed x1, local copies, waits for them, and re-layouts  1.32 us

profile of v2, /device:TPU:1, one launch (start us, length us, event | category | flops | bytes accessed | tf_op | source)
XLA Modules:
  0.0 32.4 jit_solution(124493563227356341)
XLA Ops:
  0.0 31.1 %shard_map.46 = f32[2,16,128,128]{3,2,1,0:T(8,128)S(1)} custom-call(f32[2,16,128,128]{3,2,1,0:T(8,128)} %x_hbm.1, f32[2,2,128]{2,1,0:T(2,128)} %zr_hbm.1, f32[2,2,1024]{2,1,0:T(2,128)} %mr_hbm.1, f32[2,2,128,128]{3,2,1,0:T(8,128)} %amp_hbm.1), custom_call_target="tpu_custom_call" | custom-call | tf_op jit(solution)/shard_map/pallas_call | solution.py:423
  31.1 1.3 %copy.6 = f32[2,16,128,128]{3,2,1,0:T(8,128)} copy(f32[2,16,128,128]{3,2,1,0:T(8,128)S(1)} %shard_map.46) | data formatting | bytes 4194304

commit v3 on v2

--- a/solution.py
+++ b/solution.py
@@ -90,19 +90,23 @@
 
 
 def kernel(
-    nz, nm, mem, split1, split2,
-    x_hbm, zr_hbm, mr_hbm, amp_hbm, out_ref,
-    x_ref, zr_ref, mr_ref, amp_ref, field,
-    vz_ref, vm_ref, uz_ref, um_ref,
+    nz, nm, mem, lead0, lead1, split1, split2,
+    x_hbm, zr_hbm, mr_hbm, amp_hbm,
+    field, amp_ref, uz_ref, um_ref, lq_ref, lr_ref, d_ref,
+    x_ref, zr_ref, mr_ref, vz_ref, vm_ref,
     az_wide, az_low, am_wide, am_low,
-    qs, qr, rs, rin, ps, pr, prs, pin,
-    kz_own, kz_all, km_own, km_all, crs, crr, centre,
-    lq_ref, d_ref, cr_tile,
+    qs, rin, ps, pr, prs, pin, qr, rs,
+    kz_own, kz_all, km_own, km_all, cs_own, cs_all, cz, crs, crr, centre,
+    cr_tile,
     load_sem, send_sem, recv_sem,
 ):
     zi, mi = lax.axis_index("lon"), lax.axis_index("lat")
     rows = 16 * mem
+    period = min(nz, 16)
+    near, chips, strips = period // 2, period // 2, nz // period
+    early_side = lax.rem(zi, period) < near
     zrows, mrows = rows // nz, rows // nm
+    z, core, strip = lax.rem(zi, period) // 2, lax.rem(zi, 2), zi // period
     per_pair = 4 * mem
 
     barrier = pltpu.get_barrier_semaphore()
@@ -187,8 +191,11 @@
     packed = jnp.zeros((8, 128), F32)
     for k, value in enumerate(kinds):
         packed = jnp.where(at == k, value, packed)
+    line = jnp.zeros((1, 128), F32)
     for n in range(4):
-        kz_own[n] = packed[n : n + 1]
+        mask = lane((1, 128)) // 8 == n
+        line = jnp.where(mask, pltpu.roll(packed[n : n + 1], 8 * n, 1), line)
+    kz_own[...] = line
     km_own[0:4] = packed[4:8]
     km_own[4:8] = packed[4:8]
     for f, v in enumerate((v1, v2, v3, v4)):
@@ -219,39 +226,6 @@
 
         lax.fori_loop(0, mem, states, 0, unroll=16)
 
-    pl.semaphore_wait(barrier, nz + nm - 2)
-
-    def chunk(ref, index, size):
-        return ref.at[pl.ds(pl.multiple_of(index * size, size), size), :]
-
-    def remote(src, dst, which, **device):
-        return pltpu.make_async_remote_copy(
-            src_ref=src, dst_ref=dst,
-            send_sem=send_sem.at[which], recv_sem=recv_sem.at[which],
-            device_id=device, device_id_type=MESH,
-        )
-
-    other_z, other_m = lax.rem(zi + 1, nz), lax.rem(mi + 1, nm)
-
-    def send_lon(k, _):
-        d = lax.rem(zi + k, nz)
-        remote(kz_own.at[d * zrows // per_pair], kz_all.at[zi], 1, lon=d).start()
-        remote(chunk(qs, d, zrows), chunk(qr, zi, zrows), 0, lon=d).start()
-        return 0
-
-    def send_lat(k, _):
-        d = lax.rem(mi + k, nm)
-        remote(chunk(ps, d, mrows), chunk(pr, mi, mrows), 2, lat=d).start()
-        remote(km_own, chunk(km_all, mi, 8), 3, lat=d).start()
-        return 0
-
-    lax.fori_loop(1, nz, send_lon, 0)
-    lax.fori_loop(1, nm, send_lat, 0)
-    kz_all[zi] = kz_own[zi * zrows // per_pair]
-    chunk(qr, zi, zrows)[...] = chunk(qs, zi, zrows)[...]
-    chunk(pr, mi, mrows)[...] = chunk(ps, mi, mrows)[...]
-    chunk(km_all, mi, 8)[...] = km_own[...]
-
     u3 = cols_west(ge)
     u2 = cols_west(cols_east(gw))
     u1 = cols_west(cols_east(u3))
@@ -263,22 +237,23 @@
     lit, lxt = jnp.transpose(li), jnp.transpose(lx)
     below = row(square) >= lane(square)
     above = row(square) <= lane(square)
-    for n in range(8):
-        down = jnp.where(below, lit[:, n : n + 1] - li[n : n + 1], 0.0)
-        up = jnp.where(above, lx[n : n + 1] - lxt[:, n : n + 1], 0.0)
-        east = jnp.where(below, jnp.exp(down), 0.0) * loss[n : n + 1]
-        west = jnp.where(above, jnp.exp(up), 0.0) * loss[n : n + 1]
-        once = dot3(west, east, NN)
-        high, low = halves(dot3(once, once, NN))
-        if n < 4:
-            s, l = n // 2, n % 2
-            az_wide[l, s * 128 : s * 128 + 128, 0:128] = high
-            az_wide[l, s * 128 : s * 128 + 128, 128:256] = high
-            az_low[l, s * 128 : s * 128 + 128, :] = low
-        else:
-            am_wide[n - 4, :, 0:128] = high
-            am_wide[n - 4, :, 128:256] = high
-            am_low[n - 4] = low
+    def matrices():
+        for n in range(8):
+            down = jnp.where(below, lit[:, n : n + 1] - li[n : n + 1], 0.0)
+            up = jnp.where(above, lx[n : n + 1] - lxt[:, n : n + 1], 0.0)
+            east = jnp.where(below, jnp.exp(down), 0.0) * loss[n : n + 1]
+            west = jnp.where(above, jnp.exp(up), 0.0) * loss[n : n + 1]
+            once = dot3(west, east, NN)
+            high, low = halves(dot3(once, once, NN))
+            if n < 4:
+                s, l = n // 2, n % 2
+                az_wide[l, s * 128 : s * 128 + 128, 0:128] = high
+                az_wide[l, s * 128 : s * 128 + 128, 128:256] = high
+                az_low[l, s * 128 : s * 128 + 128, :] = low
+            else:
+                am_wide[n - 4, :, 0:128] = high
+                am_wide[n - 4, :, 128:256] = high
+                am_low[n - 4] = low
 
     def local_pass(i, _):
         l, m = i // mem, lax.rem(i, mem)
@@ -292,37 +267,117 @@
             )
         return 0
 
-    lax.fori_loop(0, split1, local_pass, 0, unroll=8)
+
+    lead = jnp.where(early_side, jnp.where(z < (near + 3) // 4, lead0, lead1), 0)
+
+    @pl.when(early_side)
+    def _():
+        matrices()
+
+    def eight_passes(i, carry):
+        for j in range(8):
+            local_pass(8 * i + j, carry)
+        return carry
+
+    lax.fori_loop(0, lead, eight_passes, 0)
+
+    pl.semaphore_wait(barrier, nz + nm - 2)
+
+    def chunk(ref, index, size):
+        return ref.at[pl.ds(pl.multiple_of(index * size, size), size), :]
+
+    def remote(src, dst, which, **device):
+        return pltpu.make_async_remote_copy(
+            src_ref=src, dst_ref=dst,
+            send_sem=send_sem.at[which], recv_sem=recv_sem.at[which],
+            device_id=device, device_id_type=MESH,
+        )
+
+    other_z, other_m = lax.rem(zi + 1, nz), lax.rem(mi + 1, nm)
+
+    def sent(ref, which):
+        remote(ref, ref, which, lon=other_z).wait_send()
+
+    def landed(ref, which):
+        remote(ref, ref, which, lon=other_z).wait_recv()
+
+    def first(ref, count):
+        return ref.at[pl.ds(0, count)]
+
+    def far_first(k):
+        i = k // (2 * strips)
+        half = (i + 1) // 2
+        ahead = chips // 2 + jnp.where(lax.rem(i, 2) == 1, half, -half)
+        there = lax.rem(z + ahead, chips)
+        beside = lax.rem(core + lax.rem(k, 2), 2)
+        return lax.rem(strip + lax.rem(k // 2, strips), strips) * period + there * 2 + beside
+
+    def send_lon(k, _):
+        d = far_first(k)
+
+        @pl.when(d != zi)
+        def _():
+            remote(kz_own, kz_all.at[zi], 1, lon=d).start()
+            remote(chunk(qs, d, zrows), chunk(qr, zi, zrows), 0, lon=d).start()
+
+        return 0
+
+    def send_lat(k, _):
+        d = lax.rem(mi + k, nm)
+        remote(chunk(ps, d, mrows), chunk(pr, mi, mrows), 2, lat=d).start()
+        remote(km_own, chunk(km_all, mi, 8), 3, lat=d).start()
+        return 0
+
+    lax.fori_loop(0, nz, send_lon, 0)
+    lax.fori_loop(1, nm, send_lat, 0)
+
+    mine = jnp.concatenate(
+        [ps[pl.ds(h * 128 + f, 32, stride=4), :] for h in range(2) for f in range(4)], axis=0
+    )
+    cross = dot3(vz_ref[...], mine, NT)
+    wide = (16, rows)
+    pair_of = lane(wide) // 128 * 2 + lane(wide) // mem % 2
+    cross = jnp.where(row(wide) // 4 == pair_of, cross, 0.0)
+    cross = cross[0:4] + cross[4:8] + cross[8:12] + cross[12:16]
+    cs_own[0:4] = cross[:, 0:128]
+    cs_own[4:8] = cross[:, 128:256]
+
+    def send_states(k, _):
+        d = far_first(k)
+
+        @pl.when(d != zi)
+        def _():
+            remote(cs_own, chunk(cs_all, zi, 8), 7, lon=d).start()
+
+        return 0
+
+    lax.fori_loop(0, nz, send_states, 0)
+
+    chunk(cs_all, zi, 8)[...] = cs_own[...]
+
+    kz_all[zi] = kz_own[...]
+    chunk(qr, zi, zrows)[...] = chunk(qs, zi, zrows)[...]
+
+    chunk(pr, mi, mrows)[...] = chunk(ps, mi, mrows)[...]
+    chunk(km_all, mi, 8)[...] = km_own[...]
+
+    @pl.when(jnp.logical_not(early_side))
+    def _():
+        matrices()
+
+    lax.fori_loop(lead, jnp.maximum(lead, split1), eight_passes, 0)
 
     zshape, mshape = (nz, 128), (nm, 128)
-    remote(qs.at[pl.ds(0, (nz - 1) * zrows)], qr.at[pl.ds(0, (nz - 1) * zrows)], 0, lon=other_z).wait()
-    remote(kz_all.at[pl.ds(0, nz - 1)], kz_all.at[pl.ds(0, nz - 1)], 1, lon=other_z).wait()
-    kz = kz_all[...].reshape(nz, 128)
-    coupling = [jnp.broadcast_to(kz[:, k : k + 1], zshape) for k in range(6)]
-    groups = zrows // 4
-    got = [
-        [qr[pl.ds(g * 4 + f, nz, stride=zrows), :] for g in range(groups)] for f in range(4)
-    ]
-    for f, parts in enumerate(solve(got, coupling, nz, True)):
-        for g in range(groups):
-            rs[pl.ds(g * 4 + f, nz, stride=zrows), :] = parts[g]
-
-    def back_lon(k, _):
-        d = lax.rem(zi + k, nz)
-        remote(chunk(rs, d, zrows), chunk(rin, zi, zrows), 4, lon=d).start()
-        return 0
-
-    lax.fori_loop(1, nz, back_lon, 0)
-    chunk(rin, zi, zrows)[...] = chunk(rs, zi, zrows)[...]
-
-    remote(ps.at[pl.ds(0, (nm - 1) * mrows)], pr.at[pl.ds(0, (nm - 1) * mrows)], 2, lat=other_m).wait()
-    remote(km_all.at[pl.ds(0, (nm - 1) * 8)], km_all.at[pl.ds(0, (nm - 1) * 8)], 3, lat=other_m).wait()
+    early = lane((1, 128)) // mem % 2 == 0
+
+    landed(first(pr, (nm - 1) * mrows), 2)
+    landed(first(km_all, (nm - 1) * 8), 3)
     pair = mi * mrows // per_pair
     km = [km_all[pl.ds(n, nm, stride=8), :] for n in range(4)]
-    mine = km[0]
+    own_km = km[0]
     for n in range(1, 4):
-        mine = jnp.where(pair == n, km[n], mine)
-    coupling = [jnp.broadcast_to(mine[:, k : k + 1], mshape) for k in range(6)]
+        own_km = jnp.where(pair == n, km[n], own_km)
+    coupling = [jnp.broadcast_to(own_km[:, k : k + 1], mshape) for k in range(6)]
     groups = mrows // 4
     got = [
         [pr[pl.ds(g * 4 + f, nm, stride=mrows), :] for g in range(groups)] for f in range(4)
@@ -339,15 +394,67 @@
     lax.fori_loop(1, nm, back_lat, 0)
     chunk(pin, mi, mrows)[...] = chunk(prs, mi, mrows)[...]
 
-    lax.fori_loop(split1, split2, local_pass, 0, unroll=8)
-
-    remote(rs.at[pl.ds(0, (nz - 1) * zrows)], rin.at[pl.ds(0, (nz - 1) * zrows)], 4, lon=other_z).wait()
-    cross = dot3(vm_ref[...], rin[...], NT)
-    wide = (16, rows)
-    cross = jnp.where(row(wide) // 4 == lane(wide) // per_pair, cross, 0.0)
-    cross = cross[0:4] + cross[4:8] + cross[8:12] + cross[12:16]
-    crs[0:4] = cross[:, 0:128]
-    crs[4:8] = cross[:, 128:256]
+    lax.fori_loop(jnp.maximum(lead, split1), jnp.maximum(lead, split2), eight_passes, 0)
+
+    landed(kz_all.at[pl.ds(0, nz - 1)], 1)
+    kz = kz_all[...].reshape(nz, 128)
+    pair = zi * zrows // per_pair
+    every = [
+        [jnp.broadcast_to(kz[:, 8 * n + k : 8 * n + k + 1], zshape) for k in range(6)]
+        for n in range(4)
+    ]
+    coupling = []
+    for k in range(6):
+        value = every[0][k]
+        for n in range(1, 4):
+            value = jnp.where(pair == n, every[n][k], value)
+        coupling.append(value)
+    landed(first(qr, (nz - 1) * zrows), 0)
+    groups = zrows // 4
+    got = [
+        [qr[pl.ds(g * 4 + f, nz, stride=zrows), :] for g in range(groups)]
+        for f in range(4)
+    ]
+    for f, parts in enumerate(solve(got, coupling, nz, True)):
+        for g in range(groups):
+            rs[pl.ds(g * 4 + f, nz, stride=zrows), :] = parts[g]
+
+    def back_lon(k, _):
+        there, turn = k // (2 * strips), lax.rem(k, 2 * strips)
+        d = turn // 2 * period + there * 2 + lax.rem(turn, 2)
+
+        @pl.when(d != zi)
+        def _():
+            remote(chunk(rs, d, zrows), chunk(rin, zi, zrows), 4, lon=d).start()
+
+        return 0
+
+    lax.fori_loop(0, nz, back_lon, 0)
+    chunk(rin, zi, zrows)[...] = chunk(rs, zi, zrows)[...]
+
+
+    landed(first(cs_all, (nz - 1) * 8), 7)
+    for h in range(2):
+        coupling = [
+            jnp.where(early, every[2 * h][k], every[2 * h + 1][k]) for k in range(6)
+        ]
+        got = [[cs_all[pl.ds(h * 4 + f, nz, stride=8), :]] for f in range(4)]
+        for f, parts in enumerate(solve(got, coupling, nz, True)):
+            cz[h * 4 + f] = parts[0]
+
+    for ref, block in ((crs, zi),):
+        for h in range(2):
+            tile = jnp.concatenate(
+                [cz[h * 4 + f, pl.ds(block, 1), :] for f in range(4)] * 2, axis=0
+            )
+            turned = jnp.zeros((8, 128), F32)
+            for d in range(4):
+                moved = pltpu.roll(tile, (128 - 2 * mem * d) % 128, 1) if d else tile
+                moved = pltpu.roll(moved, d, 0) if d else moved
+                here = (row((8, 128)) - lane((8, 128)) // (2 * mem) + 8) % 4 == d
+                turned = jnp.where(here, moved, turned)
+            ref[h * 4 : h * 4 + 4, :] = turned[0:4]
+
 
     def send_cross(k, _):
         d = lax.rem(mi + k, nm)
@@ -357,9 +464,9 @@
     lax.fori_loop(1, nm, send_cross, 0)
     chunk(crr, mi, 8)[...] = crs[...]
 
-    lax.fori_loop(split2, 2 * mem, local_pass, 0, unroll=8)
-
-    remote(prs.at[pl.ds(0, (nm - 1) * mrows)], pin.at[pl.ds(0, (nm - 1) * mrows)], 5, lat=other_m).wait()
+    lax.fori_loop(jnp.maximum(lead, split2), mem // 4, eight_passes, 0)
+
+    landed(first(pin, (nm - 1) * mrows), 5)
     for n in range(4):
         s, l = n // 2, n % 2
         part = slice(n * per_pair, (n + 1) * per_pair)
@@ -367,17 +474,21 @@
         d_ref[part] = mul(
             jnp.concatenate([ph, plow], axis=1), az_wide[l, s * 128 : s * 128 + 128, :], NT
         ) + mul(ph, az_low[l, s * 128 : s * 128 + 128, :], NT)
+    amp_copy.wait()
+
+    landed(first(rin, (nz - 1) * zrows), 4)
+
+    for n in range(4):
+        part = slice(n * per_pair, (n + 1) * per_pair)
         qh, ql = halves(rin[part])
         lq_ref[part] = mul(jnp.concatenate([qh, ql], axis=1), am_wide[n], NT) + mul(
             qh, am_low[n], NT
         )
-    amp_copy.wait()
-
-    remote(crr.at[pl.ds(0, (nm - 1) * 8)], crr.at[pl.ds(0, (nm - 1) * 8)], 6, lat=other_m).wait()
+
+    landed(first(crr, (nm - 1) * 8), 6)
     for h in range(2):
-        left = lane(mshape) < per_pair
         coupling = [
-            jnp.where(left, km[2 * h][:, k : k + 1], km[2 * h + 1][:, k : k + 1])
+            jnp.where(early, km[2 * h][:, k : k + 1], km[2 * h + 1][:, k : k + 1])
             for k in range(6)
         ]
         got = [[crr[pl.ds(h * 4 + f, nm, stride=8), :]] for f in range(4)]
@@ -387,20 +498,38 @@
         h = n // 2
         for f in range(4):
             line = centre[h * 4 + f, pl.ds(mi, 1), :]
-            line = jnp.where(lane((1, 128)) // per_pair == n % 2, line, 0.0)
+            line = jnp.where(early if n % 2 == 0 else jnp.logical_not(early), line, 0.0)
             r = n * 4 + f
             cr_tile[r : r + 1, h * 128 : h * 128 + 128] = line
             cr_tile[r : r + 1, (1 - h) * 128 : (1 - h) * 128 + 128] = jnp.zeros((1, 128), F32)
-    lq_ref[...] += dot3(cr_tile[...], um_ref[...], TN)
-
-    def finish(i, _):
+    lr_ref[...] = dot3(cr_tile[...], um_ref[...], TN)
+
+    sent(first(ps, (nm - 1) * mrows), 2)
+    sent(first(km_all, (nm - 1) * 8), 3)
+    sent(first(prs, (nm - 1) * mrows), 5)
+    sent(first(crr, (nm - 1) * 8), 6)
+
+    sent(first(qs, (nz - 1) * zrows), 0)
+    sent(kz_all.at[pl.ds(0, nz - 1)], 1)
+    sent(first(rs, (nz - 1) * zrows), 4)
+
+    sent(first(cs_all, (nz - 1) * 8), 7)
+
+
+def closing(
+    mem, step, field, amp_ref, uz_ref, um_ref, lq_ref, lr_ref, d_ref, out_hbm, staged, store_sem
+):
+    per_pair = 4 * mem
+
+    def finish(i):
         l, m = i // mem, lax.rem(i, mem)
         result = None
         for s in range(2):
             n = s * 2 + l
             part = pl.ds(n * per_pair + m * 4, 4)
             resp = pl.ds(n * 4, 4)
-            left = jnp.concatenate([lq_ref[part, :], um_ref[resp, :]], axis=0)
+            entered = lr_ref[pl.ds(s * 128 + l * mem + m, 4, stride=2 * mem), :]
+            left = jnp.concatenate([lq_ref[part, :] + entered, um_ref[resp, :]], axis=0)
             right = jnp.concatenate([uz_ref[resp, :], d_ref[part, :]], axis=0)
             lh = left.astype(BF16).astype(F32)
             rh = right.astype(BF16).astype(F32)
@@ -409,47 +538,75 @@
             y = field[n, m] + mul(stacked_left, stacked_right, TN)
             y = y * amp_ref[s, l]
             result = y if result is None else result + y
-        out_ref[l, m] = result
-        return 0
-
-    lax.fori_loop(0, 2 * mem, finish, 0, unroll=8)
+        staged[l, m] = result
+
+    def put(i):
+        part = pl.ds(lax.rem(i * step, mem), step)
+        return pltpu.make_async_copy(
+            staged.at[i * step // mem, part], out_hbm.at[i * step // mem, part], store_sem.at[i]
+        )
+
+    def several(i, _):
+        for j in range(step):
+            finish(step * i + j)
+        put(i).start()
+        return 0
+
+    lax.fori_loop(0, 2 * mem // step, several, 0)
+    for i in range(2 * mem // step):
+        put(i).wait()
 
 
 def body(nz, nm, perturbations, zonal_rate, meridional_rate, amplitude):
     mem = perturbations.shape[1]
     rows = 16 * mem
     vmem = pltpu.VMEM
-    split1, split2 = 16, 24
-    return pl.pallas_call(
-        functools.partial(kernel, nz, nm, mem, split1, split2),
-        out_shape=jax.ShapeDtypeStruct(perturbations.shape, F32),
+    lead0, lead1, split1, split2 = 3, 1, 2, 3
+    pieces = pl.pallas_call(
+        functools.partial(kernel, nz, nm, mem, lead0, lead1, split1, split2),
+        out_shape=[
+            jax.ShapeDtypeStruct(shape, F32)
+            for shape in (
+                (4, mem, 128, 128), (2, 2, 128, 128), (16, 128), (16, 128),
+                (rows, 128), (rows, 128), (rows, 128),
+            )
+        ],
         in_specs=[
             pl.BlockSpec(memory_space=pltpu.HBM) for _ in range(4)
         ],
-        out_specs=pl.BlockSpec(memory_space=pltpu.VMEM),
+        out_specs=[pl.BlockSpec(memory_space=pltpu.VMEM)] * 7,
         scratch_shapes=[
             vmem((2, mem, 128, 128), F32),
             vmem((2, 2, 128), F32), vmem((2, 2, 128), F32),
-            vmem((2, 2, 128, 128), F32),
-            vmem((4, mem, 128, 128), F32),
-            vmem((16, 128), F32), vmem((16, 128), F32),
             vmem((16, 128), F32), vmem((16, 128), F32),
             vmem((2, 256, 256), BF16), vmem((2, 256, 128), BF16),
             vmem((4, 128, 256), BF16), vmem((4, 128, 128), BF16),
             *[vmem((rows, 128), F32) for _ in range(8)],
-            vmem((4, 1, 128), F32), vmem((nz, 1, 128), F32),
+            vmem((1, 128), F32), vmem((nz, 1, 128), F32),
             vmem((8, 128), F32), vmem((8 * nm, 128), F32),
+            vmem((8, 128), F32), vmem((8 * nz, 128), F32), vmem((8, nz, 128), F32),
             vmem((8, 128), F32), vmem((8 * nm, 128), F32),
             vmem((8, nm, 128), F32),
-            vmem((rows, 128), F32), vmem((rows, 128), F32), vmem((16, 256), F32),
+            vmem((16, 256), F32),
             pltpu.SemaphoreType.DMA((4,)),
-            pltpu.SemaphoreType.DMA((7,)),
-            pltpu.SemaphoreType.DMA((7,)),
+            pltpu.SemaphoreType.DMA((9,)),
+            pltpu.SemaphoreType.DMA((9,)),
         ],
         compiler_params=pltpu.CompilerParams(
             collective_id=0, has_side_effects=True, vmem_limit_bytes=48 * 1024 * 1024
         ),
     )(*(pltpu.with_memory_space_constraint(v, pltpu.HBM) for v in (perturbations, zonal_rate, meridional_rate, amplitude)))
+    step = 8
+    return pl.pallas_call(
+        functools.partial(closing, mem, step),
+        out_shape=jax.ShapeDtypeStruct(perturbations.shape, F32),
+        in_specs=[pl.BlockSpec(memory_space=pltpu.VMEM)] * 7,
+        out_specs=pl.BlockSpec(memory_space=pltpu.HBM),
+        scratch_shapes=[
+            vmem(perturbations.shape, F32), pltpu.SemaphoreType.DMA((2 * mem // step,)),
+        ],
+        compiler_params=pltpu.CompilerParams(vmem_limit_bytes=32 * 1024 * 1024),
+    )(*pieces)
 
 
 def solution(mesh):

time: 32.5 us -> 29.8 us (0.917)
  Pallas kernels: 31.1 us -> 29.7 us
  local copies, waits for them, and re-layouts: 1.32 us -> 0 us
    pallas_call x1 -> x2, Pallas kernels: 31.1 us -> 29.7 us  [the longest x1 27.5 us: body(): pl.pallas_call(functools.partial(kernel, nz, nm, mem, lead0, lead1, split...]
    unnamed x1 -> x0, local copies, waits for them, and re-layouts: 1.32 us -> none
where the time goes in v3:
time: 29.8 us; the launch traced here: 29.7 us
  Pallas kernels  29.7 us (100%)
    pallas_call x1, Pallas kernels, body(): pl.pallas_call(functools.partial(kernel, nz, nm, mem, lead0, lead1, split...  27.5 us
    pallas_call x1, Pallas kernels, body(): pl.pallas_call(functools.partial(closing, mem, step), out_shape=jax.Shape...  2.24 us

profile of v3, /device:TPU:1, one launch (start us, length us, event | category | flops | bytes accessed | tf_op | source)
XLA Modules:
  0.0 29.7 jit_solution(9769335075972178419)
XLA Ops:
  0.0 27.5 %shard_map.46 = (f32[4,16,128,128]{3,2,1,0:T(8,128)S(1)}, f32[2,2,128,128]{3,2,1,0:T(8,128)S(1)}, f32[16,128]{1,0:T(8,128)S(1)}, f32[16,128]{1,0:T(8,128)S(1)}, ...) custom-call(f32[2,16,128,128]{3,2,1,0:T(8,128)} %x_hbm.1, f32[2,2,128]{2,1,0:T(2,128)} %zr_hbm.1, ...), custom_call_target="tpu_custom_call" | custom-call | tf_op jit(solution)/shard_map/pallas_call | solution.py:565
  27.5 2.2 %shard_map.47 = f32[2,16,128,128]{3,2,1,0:T(8,128)} custom-call(f32[4,16,128,128]{3,2,1,0:T(8,128)S(1)} %get-tuple-element.12.field, f32[2,2,128,128]{3,2,1,0:T(8,128)S(1)} %get-tuple-element.13.amp_ref, f32[16,128]{1,0:T(8,128)S(1)} %get-tuple-element.14.uz_ref, f32[16,128]{1,0:T(8,128)S(1)} %get-tuple-element.15.um_ref, ...), custom_call_target="tpu_custom_call" | custom-call | tf_op jit(solution)/shard_map/pallas_call | solution.py:600

commit v4 on v3

--- a/solution.py
+++ b/solution.py
@@ -268,69 +268,6 @@
         return 0
 
 
-    lead = jnp.where(early_side, jnp.where(z < (near + 3) // 4, lead0, lead1), 0)
-
-    @pl.when(early_side)
-    def _():
-        matrices()
-
-    def eight_passes(i, carry):
-        for j in range(8):
-            local_pass(8 * i + j, carry)
-        return carry
-
-    lax.fori_loop(0, lead, eight_passes, 0)
-
-    pl.semaphore_wait(barrier, nz + nm - 2)
-
-    def chunk(ref, index, size):
-        return ref.at[pl.ds(pl.multiple_of(index * size, size), size), :]
-
-    def remote(src, dst, which, **device):
-        return pltpu.make_async_remote_copy(
-            src_ref=src, dst_ref=dst,
-            send_sem=send_sem.at[which], recv_sem=recv_sem.at[which],
-            device_id=device, device_id_type=MESH,
-        )
-
-    other_z, other_m = lax.rem(zi + 1, nz), lax.rem(mi + 1, nm)
-
-    def sent(ref, which):
-        remote(ref, ref, which, lon=other_z).wait_send()
-
-    def landed(ref, which):
-        remote(ref, ref, which, lon=other_z).wait_recv()
-
-    def first(ref, count):
-        return ref.at[pl.ds(0, count)]
-
-    def far_first(k):
-        i = k // (2 * strips)
-        half = (i + 1) // 2
-        ahead = chips // 2 + jnp.where(lax.rem(i, 2) == 1, half, -half)
-        there = lax.rem(z + ahead, chips)
-        beside = lax.rem(core + lax.rem(k, 2), 2)
-        return lax.rem(strip + lax.rem(k // 2, strips), strips) * period + there * 2 + beside
-
-    def send_lon(k, _):
-        d = far_first(k)
-
-        @pl.when(d != zi)
-        def _():
-            remote(kz_own, kz_all.at[zi], 1, lon=d).start()
-            remote(chunk(qs, d, zrows), chunk(qr, zi, zrows), 0, lon=d).start()
-
-        return 0
-
-    def send_lat(k, _):
-        d = lax.rem(mi + k, nm)
-        remote(chunk(ps, d, mrows), chunk(pr, mi, mrows), 2, lat=d).start()
-        remote(km_own, chunk(km_all, mi, 8), 3, lat=d).start()
-        return 0
-
-    lax.fori_loop(0, nz, send_lon, 0)
-    lax.fori_loop(1, nm, send_lat, 0)
-
     mine = jnp.concatenate(
         [ps[pl.ds(h * 128 + f, 32, stride=4), :] for h in range(2) for f in range(4)], axis=0
     )
@@ -341,6 +278,69 @@
     cross = cross[0:4] + cross[4:8] + cross[8:12] + cross[12:16]
     cs_own[0:4] = cross[:, 0:128]
     cs_own[4:8] = cross[:, 128:256]
+
+    lead = jnp.where(early_side, jnp.where(z < (near + 3) // 4, lead0, lead1), 0)
+
+    @pl.when(early_side)
+    def _():
+        matrices()
+
+    def eight_passes(i, carry):
+        for j in range(8):
+            local_pass(8 * i + j, carry)
+        return carry
+
+    lax.fori_loop(0, lead, eight_passes, 0)
+
+    pl.semaphore_wait(barrier, nz + nm - 2)
+
+    def chunk(ref, index, size):
+        return ref.at[pl.ds(pl.multiple_of(index * size, size), size), :]
+
+    def remote(src, dst, which, **device):
+        return pltpu.make_async_remote_copy(
+            src_ref=src, dst_ref=dst,
+            send_sem=send_sem.at[which], recv_sem=recv_sem.at[which],
+            device_id=device, device_id_type=MESH,
+        )
+
+    other_z, other_m = lax.rem(zi + 1, nz), lax.rem(mi + 1, nm)
+
+    def sent(ref, which):
+        remote(ref, ref, which, lon=other_z).wait_send()
+
+    def landed(ref, which):
+        remote(ref, ref, which, lon=other_z).wait_recv()
+
+    def first(ref, count):
+        return ref.at[pl.ds(0, count)]
+
+    def far_first(k):
+        i = k // (2 * strips)
+        half = (i + 1) // 2
+        ahead = chips // 2 + jnp.where(lax.rem(i, 2) == 1, half, -half)
+        there = lax.rem(z + ahead, chips)
+        beside = lax.rem(core + lax.rem(k, 2), 2)
+        return lax.rem(strip + lax.rem(k // 2, strips), strips) * period + there * 2 + beside
+
+    def send_lon(k, _):
+        d = far_first(k)
+
+        @pl.when(d != zi)
+        def _():
+            remote(kz_own, kz_all.at[zi], 1, lon=d).start()
+            remote(chunk(qs, d, zrows), chunk(qr, zi, zrows), 0, lon=d).start()
+
+        return 0
+
+    def send_lat(k, _):
+        d = lax.rem(mi + k, nm)
+        remote(chunk(ps, d, mrows), chunk(pr, mi, mrows), 2, lat=d).start()
+        remote(km_own, chunk(km_all, mi, 8), 3, lat=d).start()
+        return 0
+
+    lax.fori_loop(1, nm, send_lat, 0)
+    lax.fori_loop(0, nz, send_lon, 0)
 
     def send_states(k, _):
         d = far_first(k)
@@ -541,19 +541,21 @@
         staged[l, m] = result
 
     def put(i):
-        part = pl.ds(lax.rem(i * step, mem), step)
+        half = step // 2
+        part = pl.ds(lax.rem(i * half, mem), half)
         return pltpu.make_async_copy(
-            staged.at[i * step // mem, part], out_hbm.at[i * step // mem, part], store_sem.at[i]
+            staged.at[i * half // mem, part], out_hbm.at[i * half // mem, part], store_sem.at[i]
         )
 
     def several(i, _):
-        for j in range(step):
-            finish(step * i + j)
-        put(i).start()
+        for part in range(2):
+            for j in range(step // 2):
+                finish(step * i + step // 2 * part + j)
+            put(2 * i + part).start()
         return 0
 
     lax.fori_loop(0, 2 * mem // step, several, 0)
-    for i in range(2 * mem // step):
+    for i in range(4 * mem // step):
         put(i).wait()
 
 
@@ -561,7 +563,7 @@
     mem = perturbations.shape[1]
     rows = 16 * mem
     vmem = pltpu.VMEM
-    lead0, lead1, split1, split2 = 3, 1, 2, 3
+    lead0, lead1, split1, split2 = 2, 1, 2, 2
     pieces = pl.pallas_call(
         functools.partial(kernel, nz, nm, mem, lead0, lead1, split1, split2),
         out_shape=[
@@ -603,7 +605,7 @@
         in_specs=[pl.BlockSpec(memory_space=pltpu.VMEM)] * 7,
         out_specs=pl.BlockSpec(memory_space=pltpu.HBM),
         scratch_shapes=[
-            vmem(perturbations.shape, F32), pltpu.SemaphoreType.DMA((2 * mem // step,)),
+            vmem(perturbations.shape, F32), pltpu.SemaphoreType.DMA((4 * mem // step,)),
         ],
         compiler_params=pltpu.CompilerParams(vmem_limit_bytes=32 * 1024 * 1024),
     )(*pieces)

time: 29.8 us -> 29.2 us (0.980)
  Pallas kernels: 29.7 us -> 29.1 us
    pallas_call x1, Pallas kernels: 27.5 us -> 26.9 us  [body(): pl.pallas_call(functools.partial(kernel, nz, nm, mem, lead0, lead1, split...]
where the time goes in v4:
time: 29.2 us; the launch traced here: 29.1 us
  Pallas kernels  29.1 us (100%)
    pallas_call x1, Pallas kernels, body(): pl.pallas_call(functools.partial(kernel, nz, nm, mem, lead0, lead1, split...  26.9 us
    pallas_call x1, Pallas kernels, body(): pl.pallas_call(functools.partial(closing, mem, step), out_shape=jax.Shape...  2.2 us

profile of v4, /device:TPU:1, one launch (start us, length us, event | category | flops | bytes accessed | tf_op | source)
XLA Modules:
  0.0 29.1 jit_solution(14637095408579124113)
XLA Ops:
  0.0 26.9 %shard_map.46 = (f32[4,16,128,128]{3,2,1,0:T(8,128)S(1)}, f32[2,2,128,128]{3,2,1,0:T(8,128)S(1)}, f32[16,128]{1,0:T(8,128)S(1)}, f32[16,128]{1,0:T(8,128)S(1)}, ...) custom-call(f32[2,16,128,128]{3,2,1,0:T(8,128)} %x_hbm.1, f32[2,2,128]{2,1,0:T(2,128)} %zr_hbm.1, ...), custom_call_target="tpu_custom_call" | custom-call | tf_op jit(solution)/shard_map/pallas_call | solution.py:567
  26.9 2.2 %shard_map.47 = f32[2,16,128,128]{3,2,1,0:T(8,128)} custom-call(f32[4,16,128,128]{3,2,1,0:T(8,128)S(1)} %get-tuple-element.12.field, f32[2,2,128,128]{3,2,1,0:T(8,128)S(1)} %get-tuple-element.13.amp_ref, f32[16,128]{1,0:T(8,128)S(1)} %get-tuple-element.14.uz_ref, f32[16,128]{1,0:T(8,128)S(1)} %get-tuple-element.15.um_ref, ...), custom_call_target="tpu_custom_call" | custom-call | tf_op jit(solution)/shard_map/pallas_call | solution.py:602
